TPU v7x, 256 devices: a whole 4x4x8 slice. The times are simulated.
256 devices in a mesh: dp: 2 (over core), tensor: 8 (over z), expert: 16 (over y, x).
Axes of the slice: x: 4, y: 4, z: 8, core: 2. Of those that a mesh axis runs over, the one named last changes fastest.
Arguments:
- attn_heads: bfloat16 [32, 64, 4096], P(('dp', 'expert'), None, 'tensor'), may hold values from -6 to 6
- out_proj: bfloat16 [4096, 4096], P('tensor'), may hold values from -0.09375 to 0.09375
- residual: bfloat16 [32, 64, 4096], P(('dp', 'expert'), 'tensor'), may hold values from -6 to 6
- norm_gain: float32 [4096], replicated, may hold values from 0.25 to 1.75
- expert_ids: int32 [32, 64, 8], P(('dp', 'expert'), 'tensor'), may hold values from 0 to 15, all different within a row; in each aligned block of 8 rows (0 to 7, 8 to 15, ..., all dimensions but the last counted through in order) at most 6 rows name the same one
- weight_codes: int32 [32, 64, 8], P(('dp', 'expert'), 'tensor'), may hold values from 1 to 16
- w_gate: bfloat16 [16, 1536, 4096], P('expert', 'tensor'), may hold values from -0.09375 to 0.09375
- w_up: bfloat16 [16, 1536, 4096], P('expert', 'tensor'), may hold values from -0.09375 to 0.09375
- w_down: bfloat16 [16, 1536, 4096], P('expert', 'tensor'), may hold values from -0.625 to 0.625
Outputs:
- layer_out: bfloat16 [32, 64, 4096], P(('dp', 'expert'), 'tensor')
Inputs may be any that keep to these rules, and one draw needn't show every extreme that they name: `expert_ids`: each token names 8 different experts. Among the 8 consecutive tokens of one device (aligned blocks of the flattened first two dimensions) no expert is named by more than 6 rows, and every draw has an expert named exactly 6 times in some device's rows.
All inputs are finite; a program needn't handle non-finite values.
Results may differ from a plain program's by a relative error of at most 0.022.
Values may be sent and summed in bfloat16 or wider, within the bound.
No kernel may reach another device: no remote copies, remote signals or barrier semaphores. Data moves between devices by JAX's collectives and lax.ppermute only.
A program may use at most 128 MiB of HBM per device.

v0:
```python
import jax
import jax.numpy as jnp
from jax import lax
from jax.sharding import PartitionSpec as P

EXPERTS = 16
TOP = 8
CAP = 6


def normalize(hidden, norm_gain):
    mean_square = jnp.mean(hidden * hidden, axis=-1, keepdims=True)
    return (hidden * lax.rsqrt(mean_square + 1e-06) * norm_gain).astype(jnp.bfloat16)


def place_rows(route_ids, per_device):
    flat_rows = route_ids.reshape(-1)
    one_hot = (flat_rows[:, None] == jnp.arange(EXPERTS, dtype=jnp.int32)[None, :]).astype(
        jnp.int32
    )
    position = jnp.sum((jnp.cumsum(one_hot, axis=0) - one_hot) * one_hot, axis=1)
    owner_dev = flat_rows // per_device
    local_expert = flat_rows % per_device
    slot_index = owner_dev * (CAP * per_device) + position * per_device + local_expert
    return slot_index.reshape(route_ids.shape)


def build_outgoing(normed, slot_index, slot_count):
    placement = jnp.any(
        slot_index[None, :, :] == jnp.arange(slot_count, dtype=jnp.int32)[:, None, None], axis=2
    )
    return jnp.dot(
        placement.astype(jnp.bfloat16), normed, preferred_element_type=jnp.float32
    ).astype(jnp.bfloat16)


def on_device(
    attn_heads, out_proj, residual, norm_gain, expert_ids, weight_codes, w_gate, w_up, w_down
):
    tensor_count = lax.axis_size("tensor")
    expert_count = lax.axis_size("expert")
    per_device = w_gate.shape[0]
    head_rows = attn_heads[0]
    own_residual = residual[0]
    own_ids = expert_ids[0]
    own_codes = weight_codes[0]
    tok_own = own_residual.shape[0]
    model_width = own_residual.shape[1]
    slot_count = expert_count * CAP * per_device
    attn_sum = lax.psum_scatter(
        jnp.dot(head_rows, out_proj, preferred_element_type=jnp.float32).astype(jnp.bfloat16),
        "tensor",
        scatter_dimension=0,
        tiled=True,
    ).astype(jnp.float32)
    hidden = own_residual.astype(jnp.float32) + attn_sum
    normed = normalize(hidden, norm_gain)
    slot_index = place_rows(own_ids, per_device)
    outgoing = build_outgoing(normed, slot_index, slot_count).reshape(
        expert_count, CAP * per_device, model_width
    )
    arrived = lax.all_to_all(outgoing, "expert", split_axis=0, concat_axis=0, tiled=True)
    arrived = arrived.reshape(expert_count * CAP, per_device, model_width)
    portion = lax.all_gather(arrived, "tensor", axis=0, tiled=True)
    gate_value = jnp.einsum("red,efd->ref", portion, w_gate, preferred_element_type=jnp.float32)
    up_value = jnp.einsum("red,efd->ref", portion, w_up, preferred_element_type=jnp.float32)
    activated = (jax.nn.silu(gate_value) * up_value).astype(jnp.bfloat16)
    partial_out = jnp.einsum("ref,efd->red", activated, w_down, preferred_element_type=jnp.float32)
    partial_out = partial_out.astype(jnp.bfloat16).reshape(
        tensor_count * expert_count, CAP * per_device, model_width
    )
    received = lax.all_to_all(
        partial_out, ("tensor", "expert"), split_axis=0, concat_axis=0, tiled=True
    )
    received = received.reshape(tensor_count, slot_count, model_width)
    returned_flat = jnp.sum(received, axis=0, dtype=jnp.float32).astype(jnp.bfloat16)
    picked = jnp.take(returned_flat, slot_index.reshape(-1), axis=0).reshape(
        tok_own, TOP, model_width
    )
    code_values = own_codes.astype(jnp.float32)
    mixing = code_values / jnp.sum(code_values, axis=-1, keepdims=True)
    expert_mix = jnp.sum(mixing[:, :, None] * picked.astype(jnp.float32), axis=1)
    layer_out = (hidden + expert_mix).astype(jnp.bfloat16)
    return layer_out[None]


def solution(mesh):
    return jax.shard_map(
        on_device,
        mesh=mesh,
        in_specs=(
            P(("dp", "expert"), None, "tensor"),
            P("tensor", None),
            P(("dp", "expert"), "tensor", None),
            P(),
            P(("dp", "expert"), "tensor", None),
            P(("dp", "expert"), "tensor", None),
            P("expert", "tensor", None),
            P("expert", "tensor", None),
            P("expert", "tensor", None),
        ),
        out_specs=P(("dp", "expert"), "tensor", None),
        check_vma=False,
    )
```

profile of v0, /device:TPU:6, one launch (start us, length us, event | category | flops | bytes accessed | tf_op | source)
XLA Modules:
  0.0 396.0 jit_solution(4905630625477676545)
XLA Ops:
  6.5 0.0 reduce-scatter.2.cloned.1.call-start
  6.6 4.0 %convolution_convert_fusion.2 = bf16[64,4096]{1,0:T(8,128)(2,1)} fusion(bf16[512,4096]{1,0:T(8,128)(2,1)} %param.10, bf16[1,64,512]{2,1,0:T(8,128)(2,1)} %param.9), kind=kOutput, calls=%fused_computation.8 | convolution fusion | flops 268697600 | bytes 4784128 | tf_op jit(solution)/shard_map/dot_general | solution.py:51
  10.6 0.0 reduce-scatter.2.cloned.1.call-update
  10.6 0.0 all-gather.2.cloned.1.call-start
  10.6 0.1 reshape_squeeze.3
  10.7 0.1 fusion.48
  10.8 0.1 reduce_window_sum.11
  10.9 0.2 select_reduce_fusion
  11.1 0.1 reduce_sum.57
  11.2 0.1 fusion.49
  11.3 39.6 %reduce-scatter.2.cloned.1.call-done = bf16[8,4096]{1,0:T(8,128)(2,1)} async-done(((bf16[64,4096]{1,0:T(8,128)(2,1)}), bf16[8,4096]{1,0:T(8,128)(2,1)}) %reduce-scatter.2.cloned.1.call-update) | async-done | bytes 65552 | tf_op jit(solution)/shard_map/reduce_scatter | solution.py:50
  50.9 1.0 multiply_reduce_fusion.1
  51.9 1.3 convolution_convert_fusion.1
  53.1 0.3 reshape.115
  53.4 17.6 %all_to_all.10 = bf16[16,6,4096]{2,1,0:T(8,128)(2,1)} all-to-all(bf16[16,6,4096]{2,1,0:T(8,128)(2,1)S(1)} %reshape.115), channel_id=1, replica_groups=mesh['dp'=2,'tensor'=8,'expert'=16] {'expert'}, dimensions={0} | all-to-all | bytes 1572864 | tf_op jit(solution)/shard_map/all_to_all | solution.py:62
  71.0 2.2 reshape.116
  73.2 0.0 all-gather.2.cloned.1.call-update
  73.2 71.8 %all-gather.2.cloned.1.call-done = bf16[768,1,4096]{2,0,1:T(8,128)(2,1)} async-done(((bf16[96,1,4096]{2,0,1:T(8,128)(2,1)}), bf16[768,1,4096]{2,0,1:T(8,128)(2,1)}) %all-gather.2.cloned.1.call-update) | async-done | bytes 6291472 | tf_op jit(solution)/shard_map/all_gather | solution.py:64
  145.0 6.3 %fusion.8 = f32[768,1,192]{0,2,1:T(8,128)} fusion(bf16[1,192,4096]{2,1,0:T(8,128)(2,1)} %param.15, bf16[768,1,4096]{2,0,1:T(8,128)(2,1)} %all-gather.2.cloned.1.call-done), kind=kOutput, calls=%fused_computation.12 | convolution fusion | flops 1207959552 | bytes 8454144 | tf_op jit(solution)/shard_map/red,efd->ref/dot_general | solution.py:65
  151.3 13.0 %fusion.4 = bf16[768,1,4096]{2,0,1:T(8,128)(2,1)} fusion(bf16[1,192,4096]{2,1,0:T(8,128)(2,1)S(1)} %copy-done, bf16[1,192,4096]{2,1,0:T(8,128)(2,1)S(1)} %copy-done.1, bf16[768,1,4096]{2,0,1:T(8,128)(2,1)} %all-gather.2.cloned.1.call-done, f32[768,1,192]{0,2,1:T(8,128)} %fusion.8), kind=kOutput, calls=%fused_computation.6 | convolution fusion | flops 2419949568 | bytes 16318464 | tf_op jit(solution)/shard_map/ref,efd->red/dot_general | solution.py:68
  164.3 10.1 %reshape.122 = bf16[128,6,4096]{2,1,0:T(8,128)(2,1)} reshape(bf16[768,1,4096]{2,0,1:T(8,128)(2,1)} %fusion.4) | data formatting | bytes 12582912 | tf_op jit(solution)/shard_map/reshape | solution.py:69
  174.4 11.7 %all-to-all-start.1 = ((bf16[128,6,4096]{2,1,0:T(8,128)(2,1)}), bf16[128,6,4096]{2,1,0:T(8,128)(2,1)}, u32[]{:S(2)}, u32[]{:S(2)}) async-start(bf16[128,6,4096]{2,1,0:T(8,128)(2,1)} %reshape.122), calls=%async_computation.2 | async-start | bytes 16777216 | tf_op jit(solution)/shard_map/all_to_all | solution.py:72
  186.1 0.1 reduce_sum.56
  186.2 0.1 mul.72
  186.3 0.1 convert_reduce_fusion
  186.4 0.1 bitcast_divide_fusion
  186.5 186.5 %all-to-all-done.1 = bf16[128,6,4096]{2,1,0:T(8,128)(2,1)} async-done(((bf16[128,6,4096]{2,1,0:T(8,128)(2,1)}), bf16[128,6,4096]{2,1,0:T(8,128)(2,1)}, u32[]{:S(2)}, u32[]{:S(2)}) %all-to-all-start.1) | async-done | bytes 6291488 | tf_op jit(solution)/shard_map/all_to_all | solution.py:72
  373.0 10.2 %reshape.123 = bf16[8,96,4096]{2,1,0:T(8,128)(2,1)} reshape(bf16[128,6,4096]{2,1,0:T(8,128)(2,1)} %all-to-all-done.1) | data formatting | bytes 12582912 | tf_op jit(solution)/shard_map/reshape | solution.py:75
  383.2 4.0 %reduce_sum.59 = bf16[96,4096]{1,0:T(8,128)(2,1)S(1)} reduce(bf16[8,96,4096]{2,1,0:T(8,128)(2,1)} %reshape.123, bf16[]{:T(256)} %constant.65.clone.1), dimensions={0}, to_apply=%region_6.7 | reduce | flops 2752512 | bytes 7077890 | tf_op jit(solution)/shard_map/reduce_sum | solution.py:76
  387.2 0.9 gather_fusion
  388.0 0.4 multiply_reduce_fusion
  388.5 0.7 fusion.43
  (19 shorter events, 0.1 us)
Async XLA Ops:
  6.5 144.8 %copy-start = (bf16[1,192,4096]{2,1,0:T(8,128)(2,1)S(1)}, bf16[1,192,4096]{2,1,0:T(8,128)(2,1)}, u32[]{:S(2)}) copy-start(bf16[1,192,4096]{2,1,0:T(8,128)(2,1)} %param.17) | copy-start | bytes 4718596
  6.5 4.1 %copy-start.4 = (s32[1,8,8]{2,1,0:T(8,128)S(1)}, s32[1,8,8]{2,1,0:T(8,128)}, u32[]{:S(2)}) copy-start(s32[1,8,8]{2,1,0:T(8,128)} %param.13) | copy-start | bytes 772
  6.5 44.3 %copy-start.2 = (bf16[1,8,4096]{2,1,0:T(8,128)(2,1)S(1)}, bf16[1,8,4096]{2,1,0:T(8,128)(2,1)}, u32[]{:S(2)}) copy-start(bf16[1,8,4096]{2,1,0:T(8,128)(2,1)} %param.11) | copy-start | bytes 196612
  6.5 45.3 %copy-start.5 = (f32[4096]{0:T(1024)S(1)}, f32[4096]{0:T(1024)}, u32[]{:S(2)}) copy-start(f32[4096]{0:T(1024)} %param.12) | copy-start | bytes 49156
  6.5 44.3 %reduce-scatter.2.cloned.1.call-start = ((), (), s32[]{:S(2)}) async-start(), calls=%async_computation.3 | async-start | bytes 589824 | tf_op jit(solution)/shard_map/reduce_scatter | solution.py:50
  10.6 134.4 %all-gather.2.cloned.1.call-start = ((), (), s32[]{:S(2)}) async-start(), calls=%async_computation.4 | async-start | bytes 7077888 | tf_op jit(solution)/shard_map/all_gather | solution.py:64
  73.2 78.1 %copy-start.1 = (bf16[1,192,4096]{2,1,0:T(8,128)(2,1)S(1)}, bf16[1,192,4096]{2,1,0:T(8,128)(2,1)}, u32[]{:S(2)}) copy-start(bf16[1,192,4096]{2,1,0:T(8,128)(2,1)} %param.16) | copy-start | bytes 4718596
  174.4 11.9 %copy-start.6 = (s32[1,8,8]{2,1,0:T(8,128)S(1)}, s32[1,8,8]{2,1,0:T(8,128)}, u32[]{:S(2)}) copy-start(s32[1,8,8]{2,1,0:T(8,128)} %param.14) | copy-start | bytes 772
  174.4 198.5 %all-to-all-start.1 = ((bf16[128,6,4096]{2,1,0:T(8,128)(2,1)}), bf16[128,6,4096]{2,1,0:T(8,128)(2,1)}, u32[]{:S(2)}, u32[]{:S(2)}) async-start(bf16[128,6,4096]{2,1,0:T(8,128)(2,1)} %reshape.122), calls=%async_computation.2 | async-start | bytes 16777216 | tf_op jit(solution)/shard_map/all_to_all | solution.py:72
  387.1 1.3 copy-start.3
Sparse Core Ops, SparseCore 0:
  10.7 40.1 reduce-scatter.1
  73.3 71.6 all-gather.1
where the time goes:
time: 397 us; the launch traced here: 396 us
  waiting for transfers between devices  298 us (75%)
  matrix products  24.6 us (6%)
  local copies, waits for them, and re-layouts  24 us (6%)
  blocking collectives  17.6 us (4%)
  between operations  13.5 us (3%)
  starting transfers between devices  11.8 us (3%)
  other arithmetic  6.73 us (2%)
    all_to_all x1, waiting for transfers between devices, on_device(): lax.all_to_all(partial_out, ('tensor', 'expert'), split_axis=0, concat_ax...  186 us
    all_gather x1, waiting for transfers between devices, on_device(): portion = lax.all_gather(arrived, 'tensor', axis=0, tiled=True)  71.8 us
    reduce_scatter x1, waiting for transfers between devices, on_device(): lax.psum_scatter(jnp.dot(head_rows, out_proj, preferred_element_type=jnp....  39.6 us
    all_to_all x1, blocking collectives, on_device(): lax.all_to_all(outgoing, 'expert', split_axis=0, concat_axis=0, tiled=True)  17.6 us
    dot_general x1, matrix products, on_device(): jnp.einsum('ref,efd->red', activated, w_down, preferred_element_type=jnp....  13 us
    all_to_all x1, starting transfers between devices, on_device(): lax.all_to_all(partial_out, ('tensor', 'expert'), split_axis=0, concat_ax...  11.7 us
    reshape x1, local copies, waits for them, and re-layouts, on_device(): received = received.reshape(tensor_count, slot_count, model_width)  10.2 us
    reshape x1, local copies, waits for them, and re-layouts, on_device(): partial_out.astype(jnp.bfloat16)  10.1 us
  transfers between devices with their start and end apart: 3, of which 3 were waited for; matrix products, arithmetic and copies ran while one was open for 0% of the time, Pallas kernels for 0%

commit v1 on v0

--- a/solution.py
+++ b/solution.py
@@ -6,6 +6,13 @@
 EXPERTS = 16
 TOP = 8
 CAP = 6
+
+
+def gather_over(shard, name, along):
+    size = lax.axis_size(name)
+    blocks = jnp.stack([shard for _ in range(size)])
+    blocks = lax.all_to_all(blocks, name, split_axis=0, concat_axis=0)
+    return jnp.concatenate(blocks, axis=along)
 
 
 def normalize(hidden, norm_gain):
@@ -61,7 +68,7 @@
     )
     arrived = lax.all_to_all(outgoing, "expert", split_axis=0, concat_axis=0, tiled=True)
     arrived = arrived.reshape(expert_count * CAP, per_device, model_width)
-    portion = lax.all_gather(arrived, "tensor", axis=0, tiled=True)
+    portion = gather_over(arrived, "tensor", 0)
     gate_value = jnp.einsum("red,efd->ref", portion, w_gate, preferred_element_type=jnp.float32)
     up_value = jnp.einsum("red,efd->ref", portion, w_up, preferred_element_type=jnp.float32)
     activated = (jax.nn.silu(gate_value) * up_value).astype(jnp.bfloat16)

time: 397 us -> 455 us (1.15)
  blocking collectives: 17.6 us -> 157 us
  waiting for transfers between devices: 298 us -> 219 us
    all_to_all x0 -> x1, blocking collectives: none -> 140 us  [gather_over(): blocks = lax.all_to_all(blocks, name, split_axis=0, concat_axis=0)]
    all_gather x1 -> x0, waiting for transfers between devices: 71.8 us -> none  [on_device(): portion = lax.all_gather(arrived, 'tensor', axis=0, tiled=True)]
    all_to_all x1, waiting for transfers between devices: 186 us -> 180 us  [on_device(): lax.all_to_all(partial_out, ('tensor', 'expert'), split_axis=0, concat_ax...]
  transfers between devices with their start and end apart: 3 -> 2, of which waited for: 3 -> 2; matrix products, arithmetic and copies ran while one was open for 0% -> 0% of each run, Pallas kernels for 0% -> 0%
where the time goes in v1:
time: 455 us; the launch traced here: 454 us
  waiting for transfers between devices  219 us (48%)
  blocking collectives  157 us (35%)
  local copies, waits for them, and re-layouts  26.7 us (6%)
  matrix products  21.2 us (5%)
  between operations  13.5 us (3%)
  starting transfers between devices  9.76 us (2%)
  other arithmetic  6.73 us (1%)
    all_to_all x1, waiting for transfers between devices, on_device(): lax.all_to_all(partial_out, ('tensor', 'expert'), split_axis=0, concat_ax...  180 us
    all_to_all x1, blocking collectives, gather_over(): blocks = lax.all_to_all(blocks, name, split_axis=0, concat_axis=0)  140 us
    reduce_scatter x1, waiting for transfers between devices, on_device(): lax.psum_scatter(jnp.dot(head_rows, out_proj, preferred_element_type=jnp....  39.6 us
    all_to_all x1, blocking collectives, on_device(): lax.all_to_all(outgoing, 'expert', split_axis=0, concat_axis=0, tiled=True)  17.6 us
    dot_general x1, matrix products, on_device(): jnp.einsum('ref,efd->red', activated, w_down, preferred_element_type=jnp....  12.9 us
    reshape x1, local copies, waits for them, and re-layouts, on_device(): received = received.reshape(tensor_count, slot_count, model_width)  10.2 us
    reshape x1, local copies, waits for them, and re-layouts, on_device(): partial_out.astype(jnp.bfloat16)  10.1 us
    all_to_all x1, starting transfers between devices, on_device(): lax.all_to_all(partial_out, ('tensor', 'expert'), split_axis=0, concat_ax...  9.73 us
  transfers between devices with their start and end apart: 2, of which 2 were waited for; matrix products, arithmetic and copies ran while one was open for 0% of the time, Pallas kernels for 0%

profile of v1, /device:TPU:6, one launch (start us, length us, event | category | flops | bytes accessed | tf_op | source)
XLA Modules:
  0.0 454.2 jit_solution(1593618753686704789)
XLA Ops:
  6.5 0.0 reduce-scatter.2.cloned.1.call-start
  6.6 4.0 convolution_convert_fusion.2
  10.6 0.0 reduce-scatter.2.cloned.1.call-update
  10.6 0.1 reshape_squeeze.3
  10.7 0.1 fusion.29
  10.7 0.1 reduce_window_sum.11
  10.8 0.2 select_reduce_fusion
  11.0 0.1 reduce_sum.57
  11.1 0.1 fusion.30
  11.2 39.6 %reduce-scatter.2.cloned.1.call-done = bf16[8,4096]{1,0:T(8,128)(2,1)} async-done(((bf16[64,4096]{1,0:T(8,128)(2,1)}), bf16[8,4096]{1,0:T(8,128)(2,1)}) %reduce-scatter.2.cloned.1.call-update) | async-done | bytes 65552 | tf_op jit(solution)/shard_map/reduce_scatter | solution.py:57
  50.9 1.0 multiply_reduce_fusion.1
  51.9 1.3 convolution_convert_fusion.1
  53.1 0.3 reshape.119
  53.4 17.6 %all_to_all.15 = bf16[16,6,4096]{2,1,0:T(8,128)(2,1)} all-to-all(bf16[16,6,4096]{2,1,0:T(8,128)(2,1)S(1)} %reshape.119), channel_id=1, replica_groups=mesh['dp'=2,'tensor'=8,'expert'=16] {'expert'}, dimensions={0} | all-to-all | bytes 1572864 | tf_op jit(solution)/shard_map/all_to_all | solution.py:69
  71.0 1.4 stack_reshape.2
  72.4 0.8 stack.3
  73.2 139.6 %all_to_all.16 = bf16[8,96,1,4096]{3,1,2,0:T(8,128)(2,1)S(1)} all-to-all(bf16[8,96,1,4096]{3,1,2,0:T(8,128)(2,1)S(1)} %stack.3), channel_id=1, replica_groups=mesh['dp'=2,'tensor'=8,'expert'=16] {'tensor'}, dimensions={0} | all-to-all | bytes 12582912 | tf_op jit(solution)/shard_map/all_to_all | solution.py:14
  212.8 2.7 copy-done.1
  215.4 3.1 fusion.6
  218.5 12.9 %fusion = bf16[768,1,4096]{2,0,1:T(8,128)(2,1)} fusion(bf16[1,192,4096]{2,1,0:T(8,128)(2,1)S(1)} %copy-done, bf16[768,4096]{1,0:T(8,128)(2,1)} %bitcast.92, bf16[1,192,4096]{2,1,0:T(8,128)(2,1)S(1)} %copy-done.2, f32[768,1,192]{0,2,1:T(8,128)} %fusion.6), kind=kOutput, calls=%fused_computation.2 | convolution fusion | flops 2419949568 | bytes 16318464 | tf_op jit(solution)/shard_map/ref,efd->red/dot_general | solution.py:75
  231.4 10.1 %reshape.125 = bf16[128,6,4096]{2,1,0:T(8,128)(2,1)} reshape(bf16[768,1,4096]{2,0,1:T(8,128)(2,1)} %fusion) | data formatting | bytes 12582912 | tf_op jit(solution)/shard_map/reshape | solution.py:76
  241.5 9.7 %all-to-all-start.2 = ((bf16[128,6,4096]{2,1,0:T(8,128)(2,1)}), bf16[128,6,4096]{2,1,0:T(8,128)(2,1)}, u32[]{:S(2)}, u32[]{:S(2)}) async-start(bf16[128,6,4096]{2,1,0:T(8,128)(2,1)} %reshape.125), calls=%async_computation.3 | async-start | bytes 16777216 | tf_op jit(solution)/shard_map/all_to_all | solution.py:79
  251.3 0.1 reduce_sum.56
  251.4 0.1 mul.72
  251.5 0.1 convert_reduce_fusion
  251.6 0.1 bitcast_divide_fusion
  251.7 179.5 %all-to-all-done.2 = bf16[128,6,4096]{2,1,0:T(8,128)(2,1)} async-done(((bf16[128,6,4096]{2,1,0:T(8,128)(2,1)}), bf16[128,6,4096]{2,1,0:T(8,128)(2,1)}, u32[]{:S(2)}, u32[]{:S(2)}) %all-to-all-start.2) | async-done | bytes 6291488 | tf_op jit(solution)/shard_map/all_to_all | solution.py:79
  431.2 10.2 %reshape.126 = bf16[8,96,4096]{2,1,0:T(8,128)(2,1)} reshape(bf16[128,6,4096]{2,1,0:T(8,128)(2,1)} %all-to-all-done.2) | data formatting | bytes 12582912 | tf_op jit(solution)/shard_map/reshape | solution.py:82
  441.4 4.0 reduce_sum.59
  445.4 0.9 gather_fusion
  446.3 0.4 multiply_reduce_fusion
  446.7 0.7 fusion.24
  (22 shorter events, 0.1 us)
Async XLA Ops:
  6.5 212.0 %copy-start = (bf16[1,192,4096]{2,1,0:T(8,128)(2,1)S(1)}, bf16[1,192,4096]{2,1,0:T(8,128)(2,1)}, u32[]{:S(2)}) copy-start(bf16[1,192,4096]{2,1,0:T(8,128)(2,1)} %param.17) | copy-start | bytes 4718596
  6.5 4.0 copy-start.5
  6.5 44.3 %copy-start.3 = (bf16[1,8,4096]{2,1,0:T(8,128)(2,1)S(1)}, bf16[1,8,4096]{2,1,0:T(8,128)(2,1)}, u32[]{:S(2)}) copy-start(bf16[1,8,4096]{2,1,0:T(8,128)(2,1)} %param.11) | copy-start | bytes 196612
  6.5 45.3 %copy-start.6 = (f32[4096]{0:T(1024)S(1)}, f32[4096]{0:T(1024)}, u32[]{:S(2)}) copy-start(f32[4096]{0:T(1024)} %param.12) | copy-start | bytes 49156
  6.5 44.3 %reduce-scatter.2.cloned.1.call-start = ((), (), s32[]{:S(2)}) async-start(), calls=%async_computation.4 | async-start | bytes 589824 | tf_op jit(solution)/shard_map/reduce_scatter | solution.py:57
  73.2 142.2 %copy-start.8 = (bf16[1,192,4096]{2,1,0:T(8,128)(2,1)S(1)}, bf16[1,192,4096]{2,1,0:T(8,128)(2,1)}, u32[]{:S(2)}) copy-start(bf16[1,192,4096]{2,1,0:T(8,128)(2,1)} %param.15) | copy-start | bytes 4718596
  212.8 2.7 copy-start.1
  215.4 3.1 copy-start.2
  241.5 9.9 %copy-start.7 = (s32[1,8,8]{2,1,0:T(8,128)S(1)}, s32[1,8,8]{2,1,0:T(8,128)}, u32[]{:S(2)}) copy-start(s32[1,8,8]{2,1,0:T(8,128)} %param.14) | copy-start | bytes 772
  241.5 189.7 %all-to-all-start.2 = ((bf16[128,6,4096]{2,1,0:T(8,128)(2,1)}), bf16[128,6,4096]{2,1,0:T(8,128)(2,1)}, u32[]{:S(2)}, u32[]{:S(2)}) async-start(bf16[128,6,4096]{2,1,0:T(8,128)(2,1)} %reshape.125), calls=%async_computation.3 | async-start | bytes 16777216 | tf_op jit(solution)/shard_map/all_to_all | solution.py:79
  445.4 1.3 copy-start.4
Sparse Core Ops, SparseCore 0:
  10.7 40.1 reduce-scatter.1
